TPU v7x, 32 devices: a whole 2x2x4 slice. The times are simulated.
32 devices in a mesh: member: 4 (over y, x), lat: 8 (over z, core).
Axes of the slice: x: 2, y: 2, z: 4, core: 2. Of those that a mesh axis runs over, the one named last changes fastest.
Arguments:
- initial_states: float32 [4, 16, 80, 128], P('member', 'lat'), may hold values from -6 to 6
- targets: float32 [2, 16, 80, 128], P(None, 'lat'), may hold values from -6 to 6
- lat_weight: float32 [16], P('lat'), may hold values from 0.3 to 3
- weight_in: float32 [256, 720], replicated, may hold values from -0.21875 to 0.21875
- weight_out: float32 [80, 2304], replicated, may hold values from -0.125 to 0.125
- hidden_bias: float32 [256], replicated, may hold values from -4 to 4
Outputs:
- state_grad: float32 [4, 16, 80, 128], P('member', 'lat')
- loss: float32 [], replicated
All inputs are finite; a program needn't handle non-finite values.
Results may differ from a plain program's by a relative error of at most 0.00023.
Values sent between devices are 32-bit elements; how exact they have to be, the bound alone decides.
A program may use at most 64 MiB of HBM per device.

v0:
```python
import jax
import jax.numpy as jnp
from jax import lax
from jax.sharding import PartitionSpec as P

smooth_width = 0.1


def padded_2(cells, sides, width):
    for axis, dim in sides:
        count = lax.axis_size(axis)
        ends = count - 1
        head = lax.slice_in_dim(cells, 0, width, axis=dim)
        tail = lax.slice_in_dim(cells, cells.shape[dim] - width, cells.shape[dim], axis=dim)
        cells = jnp.concatenate(
            [
                lax.ppermute(tail, axis, [(i, (i + 1) % count) for i in range(ends)]),
                cells,
                lax.ppermute(head, axis, [((i + 1) % count, i) for i in range(ends)]),
            ],
            axis=dim,
        )
    return cells


def smooth(spread):
    return jnp.sqrt(spread * spread + smooth_width * smooth_width)


def convolve(matrix, padded, height, flipped):
    members = padded.shape[0]
    channels = padded.shape[2]
    columns = padded.shape[3]
    outer = matrix.shape[0]
    widened = jnp.pad(padded, ((0, 0), (0, 0), (0, 0), (1, 1)))
    blocks = matrix.reshape(outer, 9, channels)
    result = jnp.zeros((members, height, outer, columns), jnp.float32)
    for across in range(3):
        for along in range(3):
            top_row = 2 - across if flipped else across
            left_col = 2 - along if flipped else along
            window = widened[:, top_row : top_row + height, :, left_col : left_col + columns]
            result = result + jnp.einsum(
                "oc,mrcl->mrol",
                blocks[:, 3 * across + along],
                window,
                precision=lax.Precision.HIGHEST,
            )
    return result


def flip_taps(matrix, inner):
    outer = matrix.shape[0]
    return matrix.reshape(outer, 9, inner).transpose(2, 1, 0).reshape(inner, 9 * outer)


def pair_terms(mine, others, initial):

    def add_member(position, accum):
        summed, slopes = accum
        other = lax.dynamic_index_in_dim(others, position, 0, keepdims=True)
        spread = mine - other
        width = smooth(spread)
        return (summed + width, slopes + spread / width)

    return lax.fori_loop(0, others.shape[0], add_member, initial)


def on_device(initial_states, targets, lat_weight, weight_in, weight_out, hidden_bias):
    field = initial_states
    members = field.shape[0] * lax.axis_size("member")
    slab_rows = field.shape[1]
    vars_count = field.shape[2]
    columns = field.shape[3]
    hidden_count = weight_in.shape[0]
    weight_out_back = flip_taps(weight_out, hidden_count)
    weight_in_back = flip_taps(weight_in, vars_count)
    first_row = lax.axis_index("lat") * slab_rows - 1
    row_index = first_row + jnp.arange(slab_rows + 2, dtype=jnp.int32)
    inside = ((row_index >= 0) & (row_index < slab_rows * lax.axis_size("lat"))).astype(
        jnp.float32
    )[None, :, None, None]
    weights = lat_weight[None, :, None, None]
    biases = hidden_bias[None, None, :, None]
    saved = []
    loss_grads = []
    partial_value = jnp.zeros((), jnp.float32)
    for rollout in range(targets.shape[0]):
        padded = padded_2(field, (("lat", 1),), 2)
        before = convolve(weight_in, padded, slab_rows + 2, False) + biases
        hidden = jax.nn.gelu(before) * inside
        field = field + convolve(weight_out, hidden, slab_rows, False)
        saved.append(before)
        blanks = jnp.zeros_like(field)
        current = field

        def fold_pairs(accum, shards, offset, current=current):
            return pair_terms(current, shards, accum)

        summed, slopes = fold_pairs(
            (blanks, blanks), lax.all_gather(field, "member", axis=0, tiled=True), jnp.int32(0)
        )
        pair_total = jnp.sum(weights * summed)
        error = field - targets[rollout][None]
        direct = smooth(error)
        partial_value = (
            partial_value + jnp.sum(weights * direct) - pair_total / (2.0 * (members - 1))
        )
        loss_grads.append(weights * (error / direct - slopes / (members - 1)))
    overall = lax.psum(partial_value, ("member", "lat"))
    loss = overall / (
        members * targets.shape[0] * slab_rows * lax.axis_size("lat") * vars_count * columns
    )
    gradient = jnp.zeros_like(field)
    for rollout in range(targets.shape[0] - 1, -1, -1):
        gradient = gradient + loss_grads[rollout]
        before = saved[rollout]
        padded = padded_2(gradient, (("lat", 1),), 2)
        hidden_grad = convolve(weight_out_back, padded, slab_rows + 2, True) * inside
        unused, pullback = jax.vjp(jax.nn.gelu, before)
        before_grad = pullback(hidden_grad)[0]
        gradient = gradient + convolve(weight_in_back, before_grad, slab_rows, True)
    return (gradient, loss)


def solution(mesh):
    placed = (P("member", "lat", None, None), P(None, "lat", None, None), P("lat"), P(), P(), P())
    return jax.shard_map(
        on_device,
        mesh=mesh,
        in_specs=placed,
        out_specs=(P("member", "lat", None, None), P()),
        check_vma=False,
    )
```

profile of v0, /device:TPU:1, one launch (start us, length us, event | category | flops | bytes accessed | tf_op | source)
XLA Modules:
  0.0 145.4 jit_solution(14997932856672830584)
XLA Ops:
  0.6 4.6 %collective-permute-start = (f32[1,2,80,128]{3,2,1,0:T(8,128)}, f32[1,2,80,128]{3,2,1,0:T(8,128)S(1)}, u32[]{:S(2)}, u32[]{:S(2)}) collective-permute-start(f32[1,2,80,128]{3,2,1,0:T(8,128)} %param.10), channel_id=1, source_target_pairs={{0,1},{1,2},{2,3},{3,4},{4,5},{5,6},{6,7},{8,9},{9,10},{10,11},{11... | collective-permute-start | bytes 245768 | tf_op jit(solution)/shard_map/ppermute | solution.py:17
  5.2 1.9 %collective-permute-start.1 = (f32[1,2,80,128]{3,2,1,0:T(8,128)}, f32[1,2,80,128]{3,2,1,0:T(8,128)S(1)}, u32[]{:S(2)}, u32[]{:S(2)}) collective-permute-start(f32[1,2,80,128]{3,2,1,0:T(8,128)} %param.10), channel_id=1, source_target_pairs={{1,0},{2,1},{3,2},{4,3},{5,4},{6,5},{7,6},{9,8},{10,9},{11,10},{12... | collective-permute-start | bytes 245768 | tf_op jit(solution)/shard_map/ppermute | solution.py:19
  7.2 1.3 copy.176
  8.5 0.9 copy-done.1
  9.4 1.8 %collective-permute-done.1 = f32[1,2,80,128]{3,2,1,0:T(8,128)S(1)} collective-permute-done((f32[1,2,80,128]{3,2,1,0:T(8,128)}, f32[1,2,80,128]{3,2,1,0:T(8,128)S(1)}, u32[]{:S(2)}, u32[]{:S(2)}) %collective-permute-start.1) | collective-permute-done | bytes 81952 | tf_op jit(solution)/shard_map/ppermute | solution.py:19
  12.0 0.8 fusion.102
  21.2 1.0 fusion.21
  22.2 7.8 %all_gather.7 = f32[4,2,80,128]{3,2,1,0:T(8,128)S(1)} all-gather(f32[1,2,80,128]{3,2,1,0:T(8,128)} %fusion.21), channel_id=1, replica_groups=mesh['member'=4,'lat'=8] {'member'}, dimensions={0}, use_global_device_ids=true | all-gather | bytes 409600 | tf_op jit(solution)/shard_map/all_gather | solution.py:101
  30.1 4.5 %collective-permute-start.2 = (f32[1,2,80,128]{3,2,1,0:T(8,128)}, f32[1,2,80,128]{3,2,1,0:T(8,128)S(1)}, u32[]{:S(2)}, u32[]{:S(2)}) collective-permute-start(f32[1,2,80,128]{3,2,1,0:T(8,128)} %fusion.21), channel_id=1, source_target_pairs={{0,1},{1,2},{2,3},{3,4},{4,5},{5,6},{6,7},{8,9},{9,10},{10,11},{11... | collective-permute-start | bytes 245768 | tf_op jit(solution)/shard_map/ppermute | solution.py:17
  34.6 2.1 %collective-permute-start.3 = (f32[1,2,80,128]{3,2,1,0:T(8,128)}, f32[1,2,80,128]{3,2,1,0:T(8,128)S(1)}, u32[]{:S(2)}, u32[]{:S(2)}) collective-permute-start(f32[1,2,80,128]{3,2,1,0:T(8,128)} %fusion.21), channel_id=1, source_target_pairs={{1,0},{2,1},{3,2},{4,3},{5,4},{6,5},{7,6},{9,8},{10,9},{11,10},{12... | collective-permute-start | bytes 245768 | tf_op jit(solution)/shard_map/ppermute | solution.py:19
  36.7 3.9 %while.33 = (s32[]{:T(128)}, f32[1,2,80,128]{3,2,1,0:T(8,128)S(1)}, f32[1,2,80,128]{3,2,1,0:T(8,128)S(1)}, f32[4,2,80,128]{3,2,1,0:T(8,128)S(1)}, f32[1,2,80,128]{3,2,1,0:T(8,128)}, /*index=5*/s32[]{:T(128)}, s32[]{:T(128)}) while((s32[]{:T(128)}, f32[1,2,80,128]{3,2,1,0:T(8,128)S(1)}, f32[1,2,80,128]{3,2,1,0:T(8,128)S(1)}, ...), condition=%wide.region_3.4_spmd.clone, body=%wide.region_2.3_spmd.clone.sunk | while | flops 163843 | bytes 491611 | solution.py:66
  36.7 1.0 select_add_fusion.7
  37.7 1.0 select_add_fusion.7
  38.6 1.0 select_add_fusion.7
  39.6 1.0 select_add_fusion.7
  40.6 0.9 pad_maximum_fusion
  43.1 1.5 %convolution_add_fusion.20 = f32[4,128,256]{2,1,0:T(8,128)S(1)} fusion(f32[4,128,256]{2,1,0:T(8,128)S(1)} %fusion.105, f32[1,2,80,128]{3,2,1,0:T(8,128)} %fusion.21, f32[1,2,80,128]{3,2,1,0:T(8,128)S(1)} %collective-permute-done.2, f32[256,9,80]{0,2,1:T(8,128)S(1)} %bitcast.529), kind=kOutput, calls=%fused_computation.28 | convolution fusion | flops 126001152 | bytes 1294336 | tf_op jit(solution)/shard_map/oc,mrcl->mrol/dot_general | solution.py:43
  48.5 1.7 %multiply_multiply_fusion.4 = (f32[1,4,256,128]{2,3,1,0:T(8,128)S(1)}, f32[1,4,256,128]{2,3,1,0:T(8,128)S(1)}) fusion(f32[4]{0:T(128)S(1)} %and_convert_fusion, f32[256]{0:T(256)S(1)} %copy-done.3, f32[4,128,256]{2,1,0:T(8,128)S(1)} %fusion.116, f32[4,128,256]{2,1,0:T(8,128)S(1)} %convolution_add_fusion.15, f32[256,9,80]{0,2,1:T(8,128)S(1)} %bitcast.535, ...), kind=kOutput, calls=%fused_computation.134 | convolution fusion | flops 127442944 | bytes 2344448 | tf_op jit(solution)/shard_map/oc,mrcl->mrol/dot_general | solution.py:43
  53.3 1.3 fusion.22
  54.6 6.8 %all_gather.6 = f32[4,2,80,128]{3,2,1,0:T(8,128)S(1)} all-gather(f32[1,2,80,128]{3,2,1,0:T(8,128)S(1)} %fusion.22), channel_id=1, replica_groups=mesh['member'=4,'lat'=8] {'member'}, dimensions={0}, use_global_device_ids=true | all-gather | bytes 409600 | tf_op jit(solution)/shard_map/all_gather | solution.py:101
  62.4 1.7 %multiply_reduce_fusion = (f32[]{:T(128)}, f32[]{:T(128)}, f32[]{:T(128)}, f32[]{:T(128)}, f32[1,2,80,128]{3,2,1,0:T(8,128)S(1)}) fusion(f32[1,2,80,128]{3,2,1,0:T(8,128)S(1)} %get-tuple-element.195, f32[2]{0:T(128)S(1)} %copy-done.4, f32[1,2,80,128]{3,2,1,0:T(8,128)S(1)} %get-tuple-element.194, f32[1,2,80,128]{3,2,1,0:T(8,128)} %fusion.21, ...), kind=kLoop, calls=%fused_computation.300 | loop fusion | flops 368636 | bytes 655384 | tf_op jit(solution)/shard_map/reduce_sum | solution.py:103
  64.1 5.6 %collective-permute-start.4 = (f32[1,2,80,128]{3,2,1,0:T(8,128)S(1)}, f32[1,2,80,128]{3,2,1,0:T(8,128)S(1)}, u32[]{:S(2)}, u32[]{:S(2)}) collective-permute-start(f32[1,2,80,128]{3,2,1,0:T(8,128)S(1)} %get-tuple-element.264), channel_id=1, source_target_pairs={{0,1},{1,2},{2,3},{3,4},{4,5},{5,6},{6,7},{8,9},{9,10},{10,11},{11... | collective-permute-start | bytes 245768 | tf_op jit(solution)/shard_map/ppermute | solution.py:17
  69.7 2.1 %collective-permute-start.5 = (f32[1,2,80,128]{3,2,1,0:T(8,128)S(1)}, f32[1,2,80,128]{3,2,1,0:T(8,128)S(1)}, u32[]{:S(2)}, u32[]{:S(2)}) collective-permute-start(f32[1,2,80,128]{3,2,1,0:T(8,128)S(1)} %get-tuple-element.264), channel_id=1, source_target_pairs={{1,0},{2,1},{3,2},{4,3},{5,4},{6,5},{7,6},{9,8},{10,9},{11,10},{12... | collective-permute-start | bytes 245768 | tf_op jit(solution)/shard_map/ppermute | solution.py:19
  71.9 3.6 %collective-permute-done.5 = f32[1,2,80,128]{3,2,1,0:T(8,128)S(1)} collective-permute-done((f32[1,2,80,128]{3,2,1,0:T(8,128)S(1)}, f32[1,2,80,128]{3,2,1,0:T(8,128)S(1)}, u32[]{:S(2)}, u32[]{:S(2)}) %collective-permute-start.5) | collective-permute-done | bytes 81952 | tf_op jit(solution)/shard_map/ppermute | solution.py:19
  81.6 0.9 fusion.37
  85.7 1.3 fusion.24
  86.9 1.9 %collective-permute-start.6 = (f32[1,2,80,128]{3,2,1,0:T(8,128)S(1)}, f32[1,2,80,128]{3,2,1,0:T(8,128)S(1)}, u32[]{:S(2)}, u32[]{:S(2)}) collective-permute-start(f32[1,2,80,128]{3,2,1,0:T(8,128)S(1)} %fusion.24), channel_id=1, source_target_pairs={{0,1},{1,2},{2,3},{3,4},{4,5},{5,6},{6,7},{8,9},{9,10},{10,11},{11... | collective-permute-start | bytes 245768 | tf_op jit(solution)/shard_map/ppermute | solution.py:17
  88.9 2.4 %collective-permute-start.7 = (f32[1,2,80,128]{3,2,1,0:T(8,128)S(1)}, f32[1,2,80,128]{3,2,1,0:T(8,128)S(1)}, u32[]{:S(2)}, u32[]{:S(2)}) collective-permute-start(f32[1,2,80,128]{3,2,1,0:T(8,128)S(1)} %fusion.24), channel_id=1, source_target_pairs={{1,0},{2,1},{3,2},{4,3},{5,4},{6,5},{7,6},{9,8},{10,9},{11,10},{12... | collective-permute-start | bytes 245768 | tf_op jit(solution)/shard_map/ppermute | solution.py:19
  93.7 38.6 %psum.7 = f32[]{:T(128)} all-reduce(f32[]{:T(128)S(6)} %sub.49), channel_id=1, replica_groups=mesh['member'=4,'lat'=8] {'member','lat'}, use_global_device_ids=true, to_apply=%region_8.9 | all-reduce | flops 1 | bytes 8 | tf_op jit(solution)/shard_map/psum | solution.py:110
  138.4 0.8 convolution_add_fusion.1
  139.2 0.9 fusion.31
  143.2 1.0 fusion.25
  (92 shorter events, 36.3 us)
Async XLA Ops:
  0.6 7.9 %collective-permute-start = (f32[1,2,80,128]{3,2,1,0:T(8,128)}, f32[1,2,80,128]{3,2,1,0:T(8,128)S(1)}, u32[]{:S(2)}, u32[]{:S(2)}) collective-permute-start(f32[1,2,80,128]{3,2,1,0:T(8,128)} %param.10), channel_id=1, source_target_pairs={{0,1},{1,2},{2,3},{3,4},{4,5},{5,6},{6,7},{8,9},{9,10},{10,11},{11... | collective-permute-start | bytes 245768 | tf_op jit(solution)/shard_map/ppermute | solution.py:17
  5.2 6.0 %collective-permute-start.1 = (f32[1,2,80,128]{3,2,1,0:T(8,128)}, f32[1,2,80,128]{3,2,1,0:T(8,128)S(1)}, u32[]{:S(2)}, u32[]{:S(2)}) collective-permute-start(f32[1,2,80,128]{3,2,1,0:T(8,128)} %param.10), channel_id=1, source_target_pairs={{1,0},{2,1},{3,2},{4,3},{5,4},{6,5},{7,6},{9,8},{10,9},{11,10},{12... | collective-permute-start | bytes 245768 | tf_op jit(solution)/shard_map/ppermute | solution.py:19
  7.2 4.0 %copy-start = (f32[256,720]{0,1:T(8,128)S(1)}, f32[256,720]{0,1:T(8,128)}, u32[]{:S(2)}) copy-start(f32[256,720]{0,1:T(8,128)} %param.13) | copy-start | bytes 2211844
  8.5 0.9 copy-start.1
  16.5 0.8 copy-start.3
  30.1 10.5 %collective-permute-start.2 = (f32[1,2,80,128]{3,2,1,0:T(8,128)}, f32[1,2,80,128]{3,2,1,0:T(8,128)S(1)}, u32[]{:S(2)}, u32[]{:S(2)}) collective-permute-start(f32[1,2,80,128]{3,2,1,0:T(8,128)} %fusion.21), channel_id=1, source_target_pairs={{0,1},{1,2},{2,3},{3,4},{4,5},{5,6},{6,7},{8,9},{9,10},{10,11},{11... | collective-permute-start | bytes 245768 | tf_op jit(solution)/shard_map/ppermute | solution.py:17
  34.6 6.0 %collective-permute-start.3 = (f32[1,2,80,128]{3,2,1,0:T(8,128)}, f32[1,2,80,128]{3,2,1,0:T(8,128)S(1)}, u32[]{:S(2)}, u32[]{:S(2)}) collective-permute-start(f32[1,2,80,128]{3,2,1,0:T(8,128)} %fusion.21), channel_id=1, source_target_pairs={{1,0},{2,1},{3,2},{4,3},{5,4},{6,5},{7,6},{9,8},{10,9},{11,10},{12... | collective-permute-start | bytes 245768 | tf_op jit(solution)/shard_map/ppermute | solution.py:19
  61.3 0.9 copy-start.2
  61.7 0.7 copy-start.4
  64.1 7.8 %collective-permute-start.4 = (f32[1,2,80,128]{3,2,1,0:T(8,128)S(1)}, f32[1,2,80,128]{3,2,1,0:T(8,128)S(1)}, u32[]{:S(2)}, u32[]{:S(2)}) collective-permute-start(f32[1,2,80,128]{3,2,1,0:T(8,128)S(1)} %get-tuple-element.264), channel_id=1, source_target_pairs={{0,1},{1,2},{2,3},{3,4},{4,5},{5,6},{6,7},{8,9},{9,10},{10,11},{11... | collective-permute-start | bytes 245768 | tf_op jit(solution)/shard_map/ppermute | solution.py:17
  69.7 5.8 %collective-permute-start.5 = (f32[1,2,80,128]{3,2,1,0:T(8,128)S(1)}, f32[1,2,80,128]{3,2,1,0:T(8,128)S(1)}, u32[]{:S(2)}, u32[]{:S(2)}) collective-permute-start(f32[1,2,80,128]{3,2,1,0:T(8,128)S(1)} %get-tuple-element.264), channel_id=1, source_target_pairs={{1,0},{2,1},{3,2},{4,3},{5,4},{6,5},{7,6},{9,8},{10,9},{11,10},{12... | collective-permute-start | bytes 245768 | tf_op jit(solution)/shard_map/ppermute | solution.py:19
  86.9 46.1 %collective-permute-start.6 = (f32[1,2,80,128]{3,2,1,0:T(8,128)S(1)}, f32[1,2,80,128]{3,2,1,0:T(8,128)S(1)}, u32[]{:S(2)}, u32[]{:S(2)}) collective-permute-start(f32[1,2,80,128]{3,2,1,0:T(8,128)S(1)} %fusion.24), channel_id=1, source_target_pairs={{0,1},{1,2},{2,3},{3,4},{4,5},{5,6},{6,7},{8,9},{9,10},{10,11},{11... | collective-permute-start | bytes 245768 | tf_op jit(solution)/shard_map/ppermute | solution.py:17
  88.9 44.2 %collective-permute-start.7 = (f32[1,2,80,128]{3,2,1,0:T(8,128)S(1)}, f32[1,2,80,128]{3,2,1,0:T(8,128)S(1)}, u32[]{:S(2)}, u32[]{:S(2)}) collective-permute-start(f32[1,2,80,128]{3,2,1,0:T(8,128)S(1)} %fusion.24), channel_id=1, source_target_pairs={{1,0},{2,1},{3,2},{4,3},{5,4},{6,5},{7,6},{9,8},{10,9},{11,10},{12... | collective-permute-start | bytes 245768 | tf_op jit(solution)/shard_map/ppermute | solution.py:19
where the time goes:
time: 148 us; the launch traced here: 145 us
  blocking collectives  53.2 us (36%)
  matrix products  46.2 us (31%)
  starting transfers between devices  25.2 us (17%)
  other arithmetic  6.75 us (5%)
  between operations  5.61 us (4%)
  waiting for transfers between devices  5.43 us (4%)
  local copies, waits for them, and re-layouts  2.81 us (2%)
    dot_general x72, matrix products, convolve(): jnp.einsum('oc,mrcl->mrol', blocks[:, 3 * across + along], window, precis...  46.2 us
    psum x1, blocking collectives, on_device(): overall = lax.psum(partial_value, ('member', 'lat'))  38.6 us
    ppermute x4, starting transfers between devices, padded_2(): lax.ppermute(tail, axis, [(i, (i + 1) % count) for i in range(ends)])  16.6 us
    all_gather x2, blocking collectives, on_device(): lax.all_gather(field, 'member', axis=0, tiled=True)  14.6 us
    ppermute x4, starting transfers between devices, padded_2(): lax.ppermute(head, axis, [((i + 1) % count, i) for i in range(ends)])  8.57 us
    ppermute x4, waiting for transfers between devices, padded_2(): lax.ppermute(head, axis, [((i + 1) % count, i) for i in range(ends)])  5.42 us
    add x8, other arithmetic, add_member(): return (summed + width, slopes + spread / width)  4.11 us
  transfers between devices with their start and end apart: 8, of which 2 were waited for; matrix products, arithmetic and copies ran while one was open for 4% of the time, Pallas kernels for 0%

commit v1 on v0

v1 whole, which is shorter than its diff:
```python
import functools

import jax
import jax.numpy as jnp
from jax import lax
from jax.experimental import pallas as pl
from jax.experimental.pallas import tpu as pltpu
from jax.sharding import PartitionSpec as P

smooth_width = 0.1
gelu_scale = 0.7978845608028654
gelu_cubic = 0.044715
MESH = pl.DeviceIdType.MESH
F32 = jnp.float32
BF16 = jnp.bfloat16


def split(value):
    high = value.astype(BF16)
    low = (value - high.astype(F32)).astype(BF16)
    return high, low


def shifted(value, tap):
    if tap == 1:
        return value
    columns = value.shape[-1]
    lane = lax.broadcasted_iota(jnp.int32, value.shape, 1)
    if tap == 0:
        return jnp.where(lane == 0, 0.0, pltpu.roll(value, 1, 1))
    return jnp.where(lane == columns - 1, 0.0, pltpu.roll(value, columns - 1, 1))


def dot(left, right):
    return jnp.dot(left, right, preferred_element_type=F32)


def kernel(
    members, bands,
    x_ref, target_ref, lat_ref, w_in_ref, w_out_ref, bias_ref,
    grad_ref, loss_ref,
    halo, others, parts_m, parts_l, fields, grads, part_src,
    win, winb, wout, woutb, tall, wide, s_high, s_low, h_high, h_low, before, slope, loss_grad, bias,
    halo_send, halo_recv, other_send, other_recv, pm_send, pm_recv, pl_send, pl_recv,
):
    steps, rows, chans, cols = target_ref.shape
    hidden = w_in_ref.shape[0]
    taps = 3 * chans
    depth = win.shape[1]
    deep = 3 * hidden
    me_m = lax.axis_index("member")
    me_l = lax.axis_index("lat")
    has_up = me_l > 0
    has_down = me_l < bands - 1

    barrier = pltpu.get_barrier_semaphore()
    for k in range(1, members):
        pl.semaphore_signal(barrier, inc=1, device_id={"member": lax.rem(me_m + k, members)}, device_id_type=MESH)
    for k in range(1, bands):
        pl.semaphore_signal(barrier, inc=1, device_id={"lat": lax.rem(me_l + k, bands)}, device_id_type=MESH)

    @pl.when(jnp.logical_not(has_up))
    def _():
        for n in range(2 * steps):
            halo[n, 0] = jnp.zeros(halo.shape[2:], F32)

    @pl.when(jnp.logical_not(has_down))
    def _():
        for n in range(2 * steps):
            halo[n, 1] = jnp.zeros(halo.shape[2:], F32)

    def to_up(n, source):
        return pltpu.make_async_remote_copy(
            src_ref=source.at[0:2], dst_ref=halo.at[n, 1],
            send_sem=halo_send.at[n, 0], recv_sem=halo_recv.at[n, 1],
            device_id={"lat": jnp.maximum(me_l - 1, 0)}, device_id_type=MESH)

    def to_down(n, source):
        return pltpu.make_async_remote_copy(
            src_ref=source.at[rows - 2:rows], dst_ref=halo.at[n, 0],
            send_sem=halo_send.at[n, 1], recv_sem=halo_recv.at[n, 0],
            device_id={"lat": jnp.minimum(me_l + 1, bands - 1)}, device_id_type=MESH)

    def halo_start(n, source):
        @pl.when(has_up)
        def _():
            to_up(n, source).start()

        @pl.when(has_down)
        def _():
            to_down(n, source).start()

    def halo_wait(n, source):
        @pl.when(has_up)
        def _():
            to_up(n, source).wait_send()
            to_down(n, source).wait_recv()

        @pl.when(has_down)
        def _():
            to_down(n, source).wait_send()
            to_up(n, source).wait_recv()

    def to_member(step, k):
        return pltpu.make_async_remote_copy(
            src_ref=fields.at[step], dst_ref=others.at[step, k - 1],
            send_sem=other_send.at[step, k - 1], recv_sem=other_recv.at[step, k - 1],
            device_id={"member": lax.rem(me_m + k, members)}, device_id_type=MESH)

    pl.semaphore_wait(barrier, members + bands - 2)
    halo_start(0, x_ref)

    wide[:, depth - 128:depth] = jnp.zeros((hidden, 128), F32)
    wide[:, 0:3 * taps] = w_in_ref[...]
    high, low = split(wide[...])
    win[0:hidden] = high
    win[hidden:2 * hidden] = low
    for a in range(3):
        for b in range(3):
            at = (3 * a + b) * hidden
            high, low = split(w_out_ref[:, at:at + hidden])
            wout[b * chans:(b + 1) * chans, a * hidden:(a + 1) * hidden] = high
            wout[taps + b * chans:taps + (b + 1) * chans, a * hidden:(a + 1) * hidden] = low
    bias[...] = jnp.broadcast_to(bias_ref[...], (cols, hidden)).T
    tail = depth * 1 - 3 * taps
    s_high[(rows + 4) * taps:, :] = jnp.zeros((tail, cols), BF16)
    s_low[(rows + 4) * taps:, :] = jnp.zeros((tail, cols), BF16)

    def back_weights():
        tall[...] = wide[...].T
        for a in range(3):
            for b in range(3):
                at = (3 * (2 - a) + 2 - b) * chans
                high, low = split(tall[at:at + chans, :])
                winb[b * chans:(b + 1) * chans, a * hidden:(a + 1) * hidden] = high
                winb[taps + b * chans:taps + (b + 1) * chans, a * hidden:(a + 1) * hidden] = low
        for k in range(9):
            at = (8 - k) * hidden
            tall[k * chans:(k + 1) * chans, :] = w_out_ref[:, at:at + hidden]
        high, low = split(tall[...].T)
        woutb[0:hidden] = high
        woutb[hidden:2 * hidden] = low

    def widen(weights, own, n):
        for j in range(rows + 4):
            if j < 2:
                line = halo[n, 0, j]
            elif j < rows + 2:
                line = own[j - 2]
            else:
                line = halo[n, 1, j - rows - 2]
            for b in range(3):
                high, low = split(shifted(line, b))
                at = j * taps + b * chans
                s_high[at:at + chans, :] = high
                s_low[at:at + chans, :] = low
        right = jnp.concatenate([s_high[j * taps:j * taps + depth, :] for j in range(rows + 2)], axis=1)
        both = dot(weights[...], right)
        right = jnp.concatenate([s_low[j * taps:j * taps + depth, :] for j in range(rows + 2)], axis=1)
        return both[0:hidden] + both[hidden:2 * hidden] + dot(weights[0:hidden, :], right)

    def narrow(weights):
        right = jnp.concatenate([h_high[r * hidden:r * hidden + deep, :] for r in range(rows)], axis=1)
        both = dot(weights[...], right)
        right = jnp.concatenate([h_low[r * hidden:r * hidden + deep, :] for r in range(rows)], axis=1)
        total = both[0:taps] + both[taps:2 * taps] + dot(weights[0:taps, :], right)
        result = []
        for r in range(rows):
            line = total[:, r * cols:(r + 1) * cols]
            result.append(sum(shifted(line[b * chans:(b + 1) * chans], b) for b in range(3)))
        return result

    def put_hidden(j, value):
        if j == 0:
            value = jnp.where(has_up, value, 0.0)
        if j == rows + 1:
            value = jnp.where(has_down, value, 0.0)
        high, low = split(value)
        h_high[j * hidden:(j + 1) * hidden, :] = high
        h_low[j * hidden:(j + 1) * hidden, :] = low

    def fold(value):
        return sum(value[8 * i:8 * i + 8] for i in range(chans // 8))

    def loss_terms(step):
        partial = jnp.zeros((8, cols), F32)
        for r in range(rows):
            weight = lat_ref[0, r]
            mine = fields[step, r]
            error = mine - target_ref[step, r]
            square = error * error + smooth_width * smooth_width
            inverse = lax.rsqrt(square)
            direct = square * inverse
            gradient = error * inverse
            summed = jnp.full(mine.shape, smooth_width, F32)
            slopes = jnp.zeros_like(mine)
            for k in range(1, members):
                spread = mine - others[step, k - 1, r]
                square = spread * spread + smooth_width * smooth_width
                inverse = lax.rsqrt(square)
                summed = summed + square * inverse
                slopes = slopes + spread * inverse
            partial = partial + weight * fold(direct - summed / (2.0 * (members - 1)))
            loss_grad[step, r] = weight * (gradient - slopes / (members - 1))
        return partial

    for step in range(steps):
        own = x_ref if step == 0 else fields.at[step - 1]
        halo_wait(step, own)
        before[...] = widen(win, own, step)
        for j in range(rows + 2):
            value = before[:, j * cols:(j + 1) * cols] + bias[...]
            inner = jnp.tanh(gelu_scale * (value + gelu_cubic * value * value * value))
            put_hidden(j, 0.5 * value * (1.0 + inner))
            slope[step, :, j * cols:(j + 1) * cols] = 0.5 * (1.0 + inner) + 0.5 * value * (1.0 - inner * inner) * (
                gelu_scale * (1.0 + 3.0 * gelu_cubic * value * value))
        change = narrow(wout)
        for r in range(rows):
            fields[step, r] = own[r] + change[r]
        if step < steps - 1:
            halo_start(step + 1, fields.at[step])
        for k in range(1, members):
            to_member(step, k).start()
        if step == 0:
            back_weights()

    partial = jnp.zeros((8, cols), F32)
    for step in range(steps):
        for k in range(1, members):
            to_member(step, k).wait()
        partial = partial + loss_terms(step)

    def part_to_member(k):
        return pltpu.make_async_remote_copy(
            src_ref=part_src.at[0], dst_ref=parts_m.at[me_m],
            send_sem=pm_send.at[k - 1], recv_sem=pm_recv.at[me_m],
            device_id={"member": lax.rem(me_m + k, members)}, device_id_type=MESH)

    def part_from_member(k):
        source = lax.rem(me_m + k, members)
        return pltpu.make_async_remote_copy(
            src_ref=part_src.at[0], dst_ref=parts_m.at[source],
            send_sem=pm_send.at[k - 1], recv_sem=pm_recv.at[source],
            device_id={"member": source}, device_id_type=MESH)

    def part_to_band(k):
        return pltpu.make_async_remote_copy(
            src_ref=part_src.at[1], dst_ref=parts_l.at[me_l],
            send_sem=pl_send.at[k - 1], recv_sem=pl_recv.at[me_l],
            device_id={"lat": lax.rem(me_l + k, bands)}, device_id_type=MESH)

    def part_from_band(k):
        source = lax.rem(me_l + k, bands)
        return pltpu.make_async_remote_copy(
            src_ref=part_src.at[1], dst_ref=parts_l.at[source],
            send_sem=pl_send.at[k - 1], recv_sem=pl_recv.at[source],
            device_id={"lat": source}, device_id_type=MESH)

    part_src[0] = partial

    for step in range(steps - 1, -1, -1):
        n = 2 * steps - 1 - step
        own = grads.at[step]
        for r in range(rows):
            if step == steps - 1:
                grads[step, r] = loss_grad[step, r]
            else:
                grads[step, r] = grads[step + 1, r] + change[r] + loss_grad[step, r]
        halo_start(n, own)
        if step == steps - 1:
            for k in range(1, members):
                part_to_member(k).start()
            parts_m[me_m] = partial
        else:
            if step == steps - 2:
                for k in range(1, members):
                    part_to_member(k).wait_send()
                    part_from_member(k).wait_recv()
                total = sum(parts_m[k] for k in range(members))
                part_src[1] = total
                for k in range(1, bands):
                    part_to_band(k).start()
                parts_l[me_l] = total
        halo_wait(n, own)
        before[...] = widen(woutb, own, n)
        for j in range(rows + 2):
            put_hidden(j, before[:, j * cols:(j + 1) * cols] * slope[step, :, j * cols:(j + 1) * cols])
        change = narrow(winb)

    for r in range(rows):
        grad_ref[r] = grads[0, r] + change[r]
    for k in range(1, bands):
        part_to_band(k).wait_send()
        part_from_band(k).wait_recv()
    total = sum(parts_l[k] for k in range(bands))
    count = members * steps * rows * bands * chans * cols
    loss_ref[0, 0] = jnp.sum(total) / count


def on_device(members, bands, initial_states, targets, lat_weight, weight_in, weight_out, hidden_bias):
    steps, rows, chans, cols = targets.shape
    hidden = weight_in.shape[0]
    taps = 3 * chans
    depth = -(-3 * taps // 256) * 256
    deep = 3 * hidden
    vmem = pl.BlockSpec(memory_space=pltpu.VMEM)
    smem = pl.BlockSpec(memory_space=pltpu.SMEM)
    dma = pltpu.SemaphoreType.DMA
    gradient, loss = pl.pallas_call(
        functools.partial(kernel, members, bands),
        out_shape=(jax.ShapeDtypeStruct((rows, chans, cols), F32), jax.ShapeDtypeStruct((1, 1), F32)),
        in_specs=[vmem, vmem, smem, vmem, vmem, vmem],
        out_specs=(vmem, smem),
        scratch_shapes=[
            pltpu.VMEM((2 * steps, 2, 2, chans, cols), F32),
            pltpu.VMEM((steps, members - 1, rows, chans, cols), F32),
            pltpu.VMEM((members, 8, cols), F32),
            pltpu.VMEM((bands, 8, cols), F32),
            pltpu.VMEM((steps, rows, chans, cols), F32),
            pltpu.VMEM((steps, rows, chans, cols), F32),
            pltpu.VMEM((2, 8, cols), F32),
            pltpu.VMEM((2 * hidden, depth), BF16),
            pltpu.VMEM((2 * taps, deep), BF16),
            pltpu.VMEM((2 * taps, deep), BF16),
            pltpu.VMEM((2 * hidden, depth), BF16),
            pltpu.VMEM((depth, hidden), F32),
            pltpu.VMEM((hidden, depth), F32),
            pltpu.VMEM(((rows + 4) * taps + depth - 3 * taps, cols), BF16),
            pltpu.VMEM(((rows + 4) * taps + depth - 3 * taps, cols), BF16),
            pltpu.VMEM(((rows + 2) * hidden, cols), BF16),
            pltpu.VMEM(((rows + 2) * hidden, cols), BF16),
            pltpu.VMEM((hidden, (rows + 2) * cols), F32),
            pltpu.VMEM((steps, hidden, (rows + 2) * cols), F32),
            pltpu.VMEM((steps, rows, chans, cols), F32),
            pltpu.VMEM((hidden, cols), F32),
            dma((2 * steps, 2)), dma((2 * steps, 2)),
            dma((steps, members - 1)), dma((steps, members - 1)),
            dma((members - 1,)), dma((members,)),
            dma((bands - 1,)), dma((bands,)),
        ],
        compiler_params=pltpu.CompilerParams(collective_id=0, has_side_effects=True),
    )(
        initial_states.reshape(rows, chans, cols), targets, lat_weight.reshape(1, rows),
        weight_in, weight_out, hidden_bias.reshape(1, hidden),
    )
    return gradient.reshape(initial_states.shape), loss.reshape(())


def solution(mesh):
    placed = (P("member", "lat", None, None), P(None, "lat", None, None), P("lat"), P(), P(), P())
    return jax.shard_map(
        functools.partial(on_device, mesh.shape["member"], mesh.shape["lat"]),
        mesh=mesh,
        in_specs=placed,
        out_specs=(P("member", "lat", None, None), P()),
        check_vma=False,
    )
```

time: 148 us -> 39.3 us (0.27); the launches traced: 145 us -> 39 us
  blocking collectives: 53.2 us -> 0 us
  matrix products: 46.2 us -> 0 us
  Pallas kernels: 0 us -> 32.9 us
  starting transfers between devices: 25.2 us -> 0 us
  other arithmetic: 6.75 us -> 0 us
  waiting for transfers between devices: 5.43 us -> 0 us
  between operations: 5.61 us -> 2.33 us
    dot_general x72 -> x0, matrix products: 46.2 us -> none  [convolve(): jnp.einsum('oc,mrcl->mrol', blocks[:, 3 * across + along], window, precis...]
    psum x1 -> x0, blocking collectives: 38.6 us -> none  [on_device(): overall = lax.psum(partial_value, ('member', 'lat'))]
    pallas_call x0 -> x1, Pallas kernels: none -> 32.9 us  [on_device(): pl.pallas_call(functools.partial(kernel, members, bands), out_shape=(jax....]
    ppermute x8 -> x0, starting transfers between devices: 25.2 us -> none  [the longest x4 16.6 us: padded_2(): lax.ppermute(tail, axis, [(i, (i + 1) % count) for i in range(ends)])]
    all_gather x2 -> x0, blocking collectives: 14.6 us -> none  [on_device(): lax.all_gather(field, 'member', axis=0, tiled=True)]
    ppermute x8 -> x0, waiting for transfers between devices: 5.43 us -> none  [the longest x4 5.42 us: padded_2(): lax.ppermute(head, axis, [((i + 1) % count, i) for i in range(ends)])]
    add x8 -> x0, other arithmetic: 4.11 us -> none  [add_member(): return (summed + width, slopes + spread / width)]
    unnamed x12 -> x2, local copies, waits for them, and re-layouts: 1.55 us -> 3.8 us
  transfers between devices with their start and end apart: 8 -> 0, of which waited for: 2 -> 0; matrix products, arithmetic and copies ran while one was open for 4% -> 0% of each run, Pallas kernels for 0% -> 0%
where the time goes in v1:
time: 39.3 us; the launch traced here: 39 us
  Pallas kernels  32.9 us (84%)
  local copies, waits for them, and re-layouts  3.8 us (10%)
  between operations  2.33 us (6%)
    pallas_call x1, Pallas kernels, on_device(): pl.pallas_call(functools.partial(kernel, members, bands), out_shape=(jax....  32.9 us
    unnamed x2, local copies, waits for them, and re-layouts  3.8 us

profile of v1, /device:TPU:1, one launch (start us, length us, event | category | flops | bytes accessed | tf_op | source)
XLA Modules:
  0.0 39.0 jit_solution(4647333345899603956)
XLA Ops:
  0.6 2.3 %copy.8.w_in_ref = f32[256,720]{1,0:T(8,128)} copy(f32[256,720]{0,1:T(8,128)} %param.9) | data formatting | bytes 1474560 | tf_op args[3]
  2.9 32.9 %shard_map.77 = (f32[2,80,128]{2,1,0:T(8,128)}, f32[1,1]{1,0:T(1,128)}) custom-call(f32[2,80,128]{2,1,0:T(8,128)} %bitcast.5, f32[2,2,80,128]{3,2,1,0:T(8,128)} %target_ref.1, f32[1,2]{1,0:T(1,128)} %bitcast.8, f32[256,720]{1,0:T(8,128)} %copy.8.w_in_ref, f32[80,2304]{1,0:T(8,128)} %w_out_ref.1, f32[1,256]{1,0:T(1,128)} %bitcast.7), custom_call_target="tpu_custom_call" | custom-call | tf_op jit(solution)/shard_map/pallas_call | solution.py:309
  35.8 1.5 %copy.11 = f32[1,2,80,128]{3,2,1,0:T(8,128)} copy(f32[1,2,80,128]{3,2,1,0:T(8,128)} %bitcast.6) | data formatting | bytes 163840

commit v2 on v1

--- a/solution.py
+++ b/solution.py
@@ -37,28 +37,38 @@
 
 def kernel(
     members, bands,
-    x_ref, target_ref, lat_ref, w_in_ref, w_out_ref, bias_ref,
+    x_hbm, target_hbm, lat_hbm, w_in_hbm, w_out_hbm, bias_hbm,
     grad_ref, loss_ref,
+    x_ref, target_ref, lat_ref, w_in_ref, w_out_ref, bias_ref, fetch_sem,
     halo, others, parts_m, parts_l, fields, grads, part_src,
-    win, winb, wout, woutb, tall, wide, s_high, s_low, h_high, h_low, before, slope, loss_grad, bias,
+    win, winb, wout, woutb, tall, s_high, s_low, h_high, h_low, before, slope, loss_grad, bias,
     halo_send, halo_recv, other_send, other_recv, pm_send, pm_recv, pl_send, pl_recv,
 ):
     steps, rows, chans, cols = target_ref.shape
-    hidden = w_in_ref.shape[0]
+    hidden = w_in_ref.shape[1]
     taps = 3 * chans
-    depth = win.shape[1]
+    depth = win.shape[2]
     deep = 3 * hidden
     me_m = lax.axis_index("member")
     me_l = lax.axis_index("lat")
     has_up = me_l > 0
     has_down = me_l < bands - 1
 
+    fetches = [
+        pltpu.make_async_copy(source, target, fetch_sem.at[n])
+        for n, (source, target) in enumerate([
+            (x_hbm, x_ref), (w_in_hbm, w_in_ref), (w_out_hbm, w_out_ref),
+            (bias_hbm, bias_ref), (target_hbm, target_ref), (lat_hbm, lat_ref)])
+    ]
     barrier = pltpu.get_barrier_semaphore()
     for k in range(1, members):
         pl.semaphore_signal(barrier, inc=1, device_id={"member": lax.rem(me_m + k, members)}, device_id_type=MESH)
     for k in range(1, bands):
         pl.semaphore_signal(barrier, inc=1, device_id={"lat": lax.rem(me_l + k, bands)}, device_id_type=MESH)
 
+    for fetch in fetches:
+        fetch.start()
+
     @pl.when(jnp.logical_not(has_up))
     def _():
         for n in range(2 * steps):
@@ -107,57 +117,79 @@
             send_sem=other_send.at[step, k - 1], recv_sem=other_recv.at[step, k - 1],
             device_id={"member": lax.rem(me_m + k, members)}, device_id_type=MESH)
 
+    fetches[0].wait()
     pl.semaphore_wait(barrier, members + bands - 2)
     halo_start(0, x_ref)
 
-    wide[:, depth - 128:depth] = jnp.zeros((hidden, 128), F32)
-    wide[:, 0:3 * taps] = w_in_ref[...]
-    high, low = split(wide[...])
-    win[0:hidden] = high
-    win[hidden:2 * hidden] = low
-    for a in range(3):
-        for b in range(3):
-            at = (3 * a + b) * hidden
-            high, low = split(w_out_ref[:, at:at + hidden])
-            wout[b * chans:(b + 1) * chans, a * hidden:(a + 1) * hidden] = high
-            wout[taps + b * chans:taps + (b + 1) * chans, a * hidden:(a + 1) * hidden] = low
-    bias[...] = jnp.broadcast_to(bias_ref[...], (cols, hidden)).T
-    tail = depth * 1 - 3 * taps
-    s_high[(rows + 4) * taps:, :] = jnp.zeros((tail, cols), BF16)
-    s_low[(rows + 4) * taps:, :] = jnp.zeros((tail, cols), BF16)
+    def put_wide(target, a, block):
+        tall[0:taps, :] = block
+        high, low = split(tall[...].T)
+        target[a, 0:hidden] = high
+        target[a, hidden:2 * hidden] = low
+
+    def front_weights():
+        for fetch in fetches[1:]:
+            fetch.wait()
+        tall[taps:, :] = jnp.zeros((depth - taps, hidden), F32)
+        for a in range(3):
+            put_wide(win, a, w_in_ref[a * taps:(a + 1) * taps, :])
+        bias[...] = jnp.broadcast_to(bias_ref[...], (cols, hidden)).T
+        for j in range(rows + 4):
+            s_high[j * depth + taps:(j + 1) * depth, :] = jnp.zeros((depth - taps, cols), BF16)
+            s_low[j * depth + taps:(j + 1) * depth, :] = jnp.zeros((depth - taps, cols), BF16)
+
+    def narrow_weights():
+        for a in range(3):
+            for b in range(3):
+                at = (3 * a + b) * hidden
+                high, low = split(w_out_ref[:, at:at + hidden])
+                wout[b * chans:(b + 1) * chans, a * hidden:(a + 1) * hidden] = high
+                wout[taps + b * chans:taps + (b + 1) * chans, a * hidden:(a + 1) * hidden] = low
 
     def back_weights():
-        tall[...] = wide[...].T
         for a in range(3):
             for b in range(3):
                 at = (3 * (2 - a) + 2 - b) * chans
-                high, low = split(tall[at:at + chans, :])
+                high, low = split(w_in_ref[at:at + chans, :])
                 winb[b * chans:(b + 1) * chans, a * hidden:(a + 1) * hidden] = high
                 winb[taps + b * chans:taps + (b + 1) * chans, a * hidden:(a + 1) * hidden] = low
-        for k in range(9):
-            at = (8 - k) * hidden
-            tall[k * chans:(k + 1) * chans, :] = w_out_ref[:, at:at + hidden]
-        high, low = split(tall[...].T)
-        woutb[0:hidden] = high
-        woutb[hidden:2 * hidden] = low
-
-    def widen(weights, own, n):
-        for j in range(rows + 4):
-            if j < 2:
-                line = halo[n, 0, j]
-            elif j < rows + 2:
-                line = own[j - 2]
-            else:
-                line = halo[n, 1, j - rows - 2]
-            for b in range(3):
-                high, low = split(shifted(line, b))
-                at = j * taps + b * chans
-                s_high[at:at + chans, :] = high
-                s_low[at:at + chans, :] = low
-        right = jnp.concatenate([s_high[j * taps:j * taps + depth, :] for j in range(rows + 2)], axis=1)
-        both = dot(weights[...], right)
-        right = jnp.concatenate([s_low[j * taps:j * taps + depth, :] for j in range(rows + 2)], axis=1)
-        return both[0:hidden] + both[hidden:2 * hidden] + dot(weights[0:hidden, :], right)
+        for a in range(3):
+            at = 3 * (2 - a) * hidden
+            put_wide(woutb, a, jnp.concatenate(
+                [w_out_ref[:, at + (2 - b) * hidden:at + (3 - b) * hidden] for b in range(3)], axis=0))
+
+    def put_line(i, line):
+        for b in range(3):
+            high, low = split(shifted(line, b))
+            at = i * depth + b * chans
+            s_high[at:at + chans, :] = high
+            s_low[at:at + chans, :] = low
+
+    def widen_part(weights, inside):
+        sums = {}
+        for a in range(3):
+            lines = [j for j in range(rows + 2) if (2 <= j + a < rows + 2) == inside]
+            high = jnp.concatenate([s_high[(j + a) * depth:(j + a + 1) * depth, :] for j in lines], axis=1)
+            low = jnp.concatenate([s_low[(j + a) * depth:(j + a + 1) * depth, :] for j in lines], axis=1)
+            both = dot(weights[a], high)
+            total = both[0:hidden] + both[hidden:2 * hidden] + dot(weights[a, 0:hidden, :], low)
+            for n, j in enumerate(lines):
+                line = total[:, n * cols:(n + 1) * cols]
+                sums[j] = line if j not in sums else sums[j] + line
+        return sums
+
+    def widen_own(weights, own):
+        for r in range(rows):
+            put_line(r + 2, own[r])
+        for j, line in widen_part(weights, True).items():
+            before[:, j * cols:(j + 1) * cols] = line
+
+    def widen_rest(weights, n):
+        for j in range(2):
+            put_line(j, halo[n, 0, j])
+            put_line(rows + 2 + j, halo[n, 1, j])
+        for j, line in widen_part(weights, False).items():
+            before[:, j * cols:(j + 1) * cols] += line
 
     def narrow(weights):
         right = jnp.concatenate([h_high[r * hidden:r * hidden + deep, :] for r in range(rows)], axis=1)
@@ -185,7 +217,7 @@
     def loss_terms(step):
         partial = jnp.zeros((8, cols), F32)
         for r in range(rows):
-            weight = lat_ref[0, r]
+            weight = lat_ref[0:1, r:r + 1]
             mine = fields[step, r]
             error = mine - target_ref[step, r]
             square = error * error + smooth_width * smooth_width
@@ -206,8 +238,13 @@
 
     for step in range(steps):
         own = x_ref if step == 0 else fields.at[step - 1]
+        if step == 0:
+            front_weights()
+        widen_own(win, own)
+        if step == 0:
+            narrow_weights()
         halo_wait(step, own)
-        before[...] = widen(win, own, step)
+        widen_rest(win, step)
         for j in range(rows + 2):
             value = before[:, j * cols:(j + 1) * cols] + bias[...]
             inner = jnp.tanh(gelu_scale * (value + gelu_cubic * value * value * value))
@@ -281,8 +318,9 @@
                 for k in range(1, bands):
                     part_to_band(k).start()
                 parts_l[me_l] = total
+        widen_own(woutb, own)
         halo_wait(n, own)
-        before[...] = widen(woutb, own, n)
+        widen_rest(woutb, n)
         for j in range(rows + 2):
             put_hidden(j, before[:, j * cols:(j + 1) * cols] * slope[step, :, j * cols:(j + 1) * cols])
         change = narrow(winb)
@@ -301,7 +339,7 @@
     steps, rows, chans, cols = targets.shape
     hidden = weight_in.shape[0]
     taps = 3 * chans
-    depth = -(-3 * taps // 256) * 256
+    depth = -(-taps // 256) * 256
     deep = 3 * hidden
     vmem = pl.BlockSpec(memory_space=pltpu.VMEM)
     smem = pl.BlockSpec(memory_space=pltpu.SMEM)
@@ -309,9 +347,16 @@
     gradient, loss = pl.pallas_call(
         functools.partial(kernel, members, bands),
         out_shape=(jax.ShapeDtypeStruct((rows, chans, cols), F32), jax.ShapeDtypeStruct((1, 1), F32)),
-        in_specs=[vmem, vmem, smem, vmem, vmem, vmem],
+        in_specs=[pl.BlockSpec(memory_space=pl.ANY)] * 6,
         out_specs=(vmem, smem),
         scratch_shapes=[
+            pltpu.VMEM((rows, chans, cols), F32),
+            pltpu.VMEM(targets.shape, F32),
+            pltpu.VMEM((1, rows), F32),
+            pltpu.VMEM((3 * taps, hidden), F32),
+            pltpu.VMEM((chans, 3 * deep), F32),
+            pltpu.VMEM((1, hidden), F32),
+            dma((6,)),
             pltpu.VMEM((2 * steps, 2, 2, chans, cols), F32),
             pltpu.VMEM((steps, members - 1, rows, chans, cols), F32),
             pltpu.VMEM((members, 8, cols), F32),
@@ -319,14 +364,13 @@
             pltpu.VMEM((steps, rows, chans, cols), F32),
             pltpu.VMEM((steps, rows, chans, cols), F32),
             pltpu.VMEM((2, 8, cols), F32),
-            pltpu.VMEM((2 * hidden, depth), BF16),
+            pltpu.VMEM((3, 2 * hidden, depth), BF16),
             pltpu.VMEM((2 * taps, deep), BF16),
             pltpu.VMEM((2 * taps, deep), BF16),
-            pltpu.VMEM((2 * hidden, depth), BF16),
+            pltpu.VMEM((3, 2 * hidden, depth), BF16),
             pltpu.VMEM((depth, hidden), F32),
-            pltpu.VMEM((hidden, depth), F32),
-            pltpu.VMEM(((rows + 4) * taps + depth - 3 * taps, cols), BF16),
-            pltpu.VMEM(((rows + 4) * taps + depth - 3 * taps, cols), BF16),
+            pltpu.VMEM(((rows + 4) * depth, cols), BF16),
+            pltpu.VMEM(((rows + 4) * depth, cols), BF16),
             pltpu.VMEM(((rows + 2) * hidden, cols), BF16),
             pltpu.VMEM(((rows + 2) * hidden, cols), BF16),
             pltpu.VMEM((hidden, (rows + 2) * cols), F32),
@@ -341,7 +385,7 @@
         compiler_params=pltpu.CompilerParams(collective_id=0, has_side_effects=True),
     )(
         initial_states.reshape(rows, chans, cols), targets, lat_weight.reshape(1, rows),
-        weight_in, weight_out, hidden_bias.reshape(1, hidden),
+        weight_in.T, weight_out, hidden_bias.reshape(1, hidden),
     )
     return gradient.reshape(initial_states.shape), loss.reshape(())
 

time: 39.3 us -> 33.3 us (0.85)
  Pallas kernels: 32.9 us -> 29.1 us
  local copies, waits for them, and re-layouts: 3.8 us -> 1.53 us
    pallas_call x1, Pallas kernels: 32.9 us -> 29.1 us  [on_device(): pl.pallas_call(functools.partial(kernel, members, bands), out_shape=(jax....]
    unnamed x2 -> x1, local copies, waits for them, and re-layouts: 3.8 us -> 1.53 us
where the time goes in v2:
time: 33.3 us; the launch traced here: 33 us
  Pallas kernels  29.1 us (87%)
  between operations  2.33 us (7%)
  local copies, waits for them, and re-layouts  1.53 us (5%)
    pallas_call x1, Pallas kernels, on_device(): pl.pallas_call(functools.partial(kernel, members, bands), out_shape=(jax....  29.1 us
    unnamed x1, local copies, waits for them, and re-layouts  1.53 us

profile of v2, /device:TPU:1, one launch (start us, length us, event | category | flops | bytes accessed | tf_op | source)
XLA Modules:
  0.0 33.0 jit_solution(12750036125039101865)
XLA Ops:
  0.6 29.1 %shard_map.77 = (f32[2,80,128]{2,1,0:T(8,128)}, f32[1,1]{1,0:T(1,128)}) custom-call(f32[2,80,128]{2,1,0:T(8,128)} %bitcast.7, f32[2,2,80,128]{3,2,1,0:T(8,128)} %target_hbm.1, f32[1,2]{1,0:T(1,128)} %bitcast.10, f32[720,256]{1,0:T(8,128)} %bitcast.6, f32[80,2304]{1,0:T(8,128)} %w_out_hbm.1, f32[1,256]{1,0:T(1,128)} %bitcast.9), custom_call_target="tpu_custom_call" | custom-call | tf_op jit(solution)/shard_map/pallas_call | solution.py:347
  29.8 1.5 %copy.10 = f32[1,2,80,128]{3,2,1,0:T(8,128)} copy(f32[1,2,80,128]{3,2,1,0:T(8,128)} %bitcast.8) | data formatting | bytes 163840

commit v3 on v2

--- a/solution.py
+++ b/solution.py
@@ -217,23 +217,21 @@
     def loss_terms(step):
         partial = jnp.zeros((8, cols), F32)
         for r in range(rows):
-            weight = lat_ref[0:1, r:r + 1]
-            mine = fields[step, r]
-            error = mine - target_ref[step, r]
+            error = fields[step, r] - target_ref[step, r]
             square = error * error + smooth_width * smooth_width
             inverse = lax.rsqrt(square)
-            direct = square * inverse
-            gradient = error * inverse
-            summed = jnp.full(mine.shape, smooth_width, F32)
-            slopes = jnp.zeros_like(mine)
-            for k in range(1, members):
-                spread = mine - others[step, k - 1, r]
+            scale = lat_ref[0:1, r:r + 1]
+            partial = partial + scale * fold(square * inverse - smooth_width / (2.0 * (members - 1)))
+            loss_grad[step, r] = scale * (error * inverse)
+        for k in range(1, members):
+            to_member(step, k).wait()
+            for r in range(rows):
+                spread = fields[step, r] - others[step, k - 1, r]
                 square = spread * spread + smooth_width * smooth_width
                 inverse = lax.rsqrt(square)
-                summed = summed + square * inverse
-                slopes = slopes + spread * inverse
-            partial = partial + weight * fold(direct - summed / (2.0 * (members - 1)))
-            loss_grad[step, r] = weight * (gradient - slopes / (members - 1))
+                scale = lat_ref[0:1, r:r + 1]
+                partial = partial - scale / (2.0 * (members - 1)) * fold(square * inverse)
+                loss_grad[step, r] = loss_grad[step, r] - scale / (members - 1) * (spread * inverse)
         return partial
 
     for step in range(steps):
@@ -263,8 +261,6 @@
 
     partial = jnp.zeros((8, cols), F32)
     for step in range(steps):
-        for k in range(1, members):
-            to_member(step, k).wait()
         partial = partial + loss_terms(step)
 
     def part_to_member(k):

time: 33.3 us -> 33.3 us (level)
  no operation moved by 1% of the time
where the time goes in v3:
time: 33.3 us; the launch traced here: 33 us
  Pallas kernels  29.2 us (88%)
  between operations  2.33 us (7%)
  local copies, waits for them, and re-layouts  1.53 us (5%)
    pallas_call x1, Pallas kernels, on_device(): pl.pallas_call(functools.partial(kernel, members, bands), out_shape=(jax....  29.2 us
    unnamed x1, local copies, waits for them, and re-layouts  1.53 us

profile of v3, /device:TPU:1, one launch (start us, length us, event | category | flops | bytes accessed | tf_op | source)
XLA Modules:
  0.0 33.0 jit_solution(13075834120738919513)
XLA Ops:
  0.6 29.2 %shard_map.77 = (f32[2,80,128]{2,1,0:T(8,128)}, f32[1,1]{1,0:T(1,128)}) custom-call(f32[2,80,128]{2,1,0:T(8,128)} %bitcast.7, f32[2,2,80,128]{3,2,1,0:T(8,128)} %target_hbm.1, f32[1,2]{1,0:T(1,128)} %bitcast.10, f32[720,256]{1,0:T(8,128)} %bitcast.6, f32[80,2304]{1,0:T(8,128)} %w_out_hbm.1, f32[1,256]{1,0:T(1,128)} %bitcast.9), custom_call_target="tpu_custom_call" | custom-call | tf_op jit(solution)/shard_map/pallas_call | solution.py:343
  29.8 1.5 %copy.10 = f32[1,2,80,128]{3,2,1,0:T(8,128)} copy(f32[1,2,80,128]{3,2,1,0:T(8,128)} %bitcast.8) | data formatting | bytes 163840
